TPU v7x, 32 devices: a whole 2x2x4 slice. The times are simulated.
32 devices in a mesh: dp: 16 (over z, y, core), own: 2 (over x).
Axes of the slice: x: 2, y: 2, z: 4, core: 2. Of those that a mesh axis runs over, the one named last changes fastest.
Arguments:
- layer_inputs: bfloat16 [4, 16, 16, 128, 128], P(None, 'dp', 'own'), as said below
- weights: bfloat16 [4, 1152, 128], replicated, may hold values from -0.1875 to 0.1875
- top_cotangent: bfloat16 [16, 16, 128, 128], P('dp', 'own'), may hold values from -6 to 6
- segmentation: int32 [16, 16, 128], P('dp', 'own'), may hold values from 0 to 2
- layer_slots: int32 [4], replicated, may hold values from 0 to 3, as said below
- a_inverse: bfloat16 [4, 1152, 1152], P('own', 'dp'), as said below
- g_inverse: bfloat16 [4, 128, 128], P('own'), as said below
Outputs:
- preconditioned: float32 [4, 1152, 128], P(None, 'dp')
- input_grad: bfloat16 [16, 16, 128, 128], P('dp', 'own')
Inputs may be any that keep to these rules, and one draw needn't show every extreme that they name: Distinct slot numbers; layer l is held by owner layer_slots[l] // 2, in that owner's slot layer_slots[l] % 2. One owner holds exactly 2 layers in every draw. `a_inverse`: each factor is symmetric. `g_inverse`: each factor is symmetric. `layer_inputs`: activations after a rectifier.
All inputs are finite; a program needn't handle non-finite values.
Results may differ from a plain program's by a relative error of at most 0.011.
Values may be sent and summed in bfloat16 or wider, within the bound.
A program may use at most 64 MiB of HBM per device.

v0:
```python
import math

import jax
import jax.numpy as jnp
from jax import lax
from jax.sharding import PartitionSpec as P


def extended(cells, sides, width):
    for axis, dim in sides:
        count = lax.axis_size(axis)
        ends = count - 1
        head = lax.slice_in_dim(cells, 0, width, axis=dim)
        tail = lax.slice_in_dim(cells, cells.shape[dim] - width, cells.shape[dim], axis=dim)
        cells = jnp.concatenate(
            [
                lax.ppermute(tail, axis, [(i, (i + 1) % count) for i in range(ends)]),
                cells,
                lax.ppermute(head, axis, [((i + 1) % count, i) for i in range(ends)]),
            ],
            axis=dim,
        )
    return cells


def from_root(block, axis, owner):
    block = jnp.where(lax.axis_index(axis) == owner, block, jnp.zeros_like(block))
    return lax.psum(block, axis)


def loss_weight(labels):
    return jnp.where(labels == 0, 1.0, jnp.where(labels == 1, 0.0, 0.5)).astype(jnp.float32)


def tap_matrix(padded, num_rows, num_cols):
    channels = padded.shape[-1]
    pieces = []
    for tap_index in range(9):
        row_start = 2 - tap_index // 3
        col_start = 2 - tap_index % 3
        pieces.append(padded[row_start : row_start + num_rows, col_start : col_start + num_cols])
    stacked = jnp.stack(pieces, axis=2)
    return stacked.reshape(num_rows * num_cols, 9 * channels)


def per_device(
    layer_inputs, weights, top_cotangent, segmentation, layer_slots, a_inverse, g_inverse
):
    layer_count = layer_inputs.shape[0]
    num_rows = layer_inputs.shape[2]
    num_cols = layer_inputs.shape[3]
    channels = layer_inputs.shape[4]
    data_devices = lax.axis_size("dp")
    owner_devices = lax.axis_size("own")
    grad_scale = 1.0 / math.sqrt(data_devices * owner_devices * num_rows * num_cols)
    inputs_local = layer_inputs[:, 0]
    scaled = loss_weight(segmentation[0])[:, :, None] * top_cotangent[0].astype(jnp.float32)
    out_grad = scaled.astype(jnp.bfloat16)
    grad_blocks = [None] * layer_count
    input_grad = None
    for layer_index in range(layer_count - 1, -1, -1):
        rimmed = extended(out_grad, (("own", 0),), 1)
        padded = jnp.pad(rimmed, ((0, 0), (1, 1), (0, 0)))
        tap_rows = tap_matrix(padded, num_rows, num_cols)
        flat_inputs = inputs_local[layer_index].reshape(num_rows * num_cols, channels)
        grad_block = lax.dot_general(
            flat_inputs, tap_rows, (((0,), (0,)), ((), ())), preferred_element_type=jnp.float32
        )
        grad_blocks[layer_index] = grad_block.reshape(9 * channels, channels) * grad_scale
        kernel = weights[layer_index].reshape(channels, 9 * channels)
        input_side = lax.dot_general(
            tap_rows, kernel, (((1,), (1,)), ((), ())), preferred_element_type=jnp.float32
        )
        input_side = input_side.reshape(num_rows, num_cols, channels)
        if layer_index > 0:
            out_grad = jnp.where(inputs_local[layer_index] > 0, input_side, 0.0).astype(
                jnp.bfloat16
            )
        else:
            input_grad = input_side.astype(jnp.bfloat16)[None]
    grad_term = jnp.concatenate(grad_blocks, axis=1)
    grad_rows = lax.psum_scatter(grad_term, "dp", scatter_dimension=0, tiled=True)
    slot_count = a_inverse.shape[0]
    grad_sum = lax.psum(grad_rows.astype(jnp.bfloat16), "own")
    left_panels = []
    right_panels = []
    for layer_index in range(layer_count):
        slot_id = layer_slots[layer_index]
        owner_index = slot_id // slot_count
        local_slot = slot_id % slot_count
        left_panel = lax.dynamic_index_in_dim(a_inverse, local_slot, 0, keepdims=False)
        right_panel = lax.dynamic_index_in_dim(g_inverse, local_slot, 0, keepdims=False)
        left_panel, right_panel = (
            from_root(left_panel, "own", owner_index),
            from_root(right_panel, "own", owner_index),
        )
        left_panels.append(left_panel)
        right_panels.append(right_panel)
    left_stack = jnp.stack(left_panels, axis=0)
    right_stack = jnp.stack(right_panels, axis=0)
    gathered_piece = lax.all_gather(grad_sum, "dp", axis=0, tiled=True)
    width_here = gathered_piece.shape[0]
    shaped_piece = gathered_piece.reshape(width_here, layer_count, channels)
    left_product = jnp.einsum(
        "lrn,nlc->lrc", left_stack, shaped_piece, preferred_element_type=jnp.float32
    )
    preconditioned = jnp.einsum(
        "lrc,lcd->lrd",
        left_product.astype(jnp.bfloat16),
        right_stack,
        preferred_element_type=jnp.float32,
    )
    return (preconditioned, input_grad)


def solution(mesh):
    in_specs = (
        P(None, "dp", "own", None, None),
        P(),
        P("dp", "own", None, None),
        P("dp", "own", None),
        P(),
        P("own", "dp", None),
        P("own", None, None),
    )
    out_specs = (P(None, "dp", None), P("dp", "own", None, None))
    return jax.shard_map(
        per_device, mesh=mesh, in_specs=in_specs, out_specs=out_specs, check_vma=False
    )
```

profile of v0, /device:TPU:0, one launch (start us, length us, event | category | flops | bytes accessed | tf_op | source)
XLA Modules:
  0.0 266.4 jit_solution(8736624988374941266)
XLA Ops:
  9.2 1.3 collective-permute-start.1
  10.5 4.8 %collective-permute-start = (bf16[1,128,128]{1,2,0:T(8,128)(2,1)S(1)}, bf16[1,128,128]{1,2,0:T(8,128)(2,1)S(1)}, u32[]{:S(2)}, u32[]{:S(2)}) collective-permute-start(bf16[1,128,128]{1,2,0:T(8,128)(2,1)S(1)} %get-tuple-element.29), channel_id=1, source_target_pairs={{0,1},{2,3},{4,5},{6,7},{8,9},{10,11},{12,13},{14,15},{16,17},{18,... | collective-permute-start | bytes 98312 | tf_op jit(solution)/shard_map/ppermute | solution.py:17
  15.4 1.3 fusion.111
  21.5 1.6 copy.30
  23.1 1.8 fusion.13
  26.9 5.1 %collective-permute-start.2 = (bf16[1,128,128]{2,1,0:T(8,128)(2,1)}, bf16[1,128,128]{2,1,0:T(8,128)(2,1)S(1)}, u32[]{:S(2)}, u32[]{:S(2)}) collective-permute-start(bf16[1,128,128]{2,1,0:T(8,128)(2,1)} %get-tuple-element.27), channel_id=1, source_target_pairs={{0,1},{2,3},{4,5},{6,7},{8,9},{10,11},{12,13},{14,15},{16,17},{18,... | collective-permute-start | bytes 98312 | tf_op jit(solution)/shard_map/ppermute | solution.py:17
  36.1 2.7 copy.28
  38.8 2.5 copy.20
  41.2 2.7 %fusion.14 = bf16[8,128,128]{2,1,0:T(8,128)(2,1)S(1)} fusion(bf16[8,128,1152]{1,2,0:T(8,128)(2,1)} %bitcast.255, bf16[128,1152,1]{1,0,2:T(8,128)(2,1)} %reshape.135, bf16[4,1,8,128,128]{4,3,2,1,0:T(8,128)(2,1)} %param.7), kind=kOutput, calls=%fused_computation.24 | convolution fusion | flops 302383104 | bytes 3178496 | tf_op jit(solution)/shard_map/dot_general | solution.py:71
  44.6 1.3 collective-permute-start.5
  45.9 5.3 %collective-permute-start.4 = (bf16[1,128,128]{2,1,0:T(8,128)(2,1)}, bf16[1,128,128]{2,1,0:T(8,128)(2,1)S(1)}, u32[]{:S(2)}, u32[]{:S(2)}) collective-permute-start(bf16[1,128,128]{2,1,0:T(8,128)(2,1)} %get-tuple-element.25), channel_id=1, source_target_pairs={{0,1},{2,3},{4,5},{6,7},{8,9},{10,11},{12,13},{14,15},{16,17},{18,... | collective-permute-start | bytes 98312 | tf_op jit(solution)/shard_map/ppermute | solution.py:17
  51.2 1.6 fusion.2
  52.8 1.3 copy.29
  57.2 2.7 copy.26
  59.9 2.5 copy.22
  62.3 2.7 %fusion.15 = bf16[8,128,128]{2,1,0:T(8,128)(2,1)S(1)} fusion(bf16[8,128,1152]{1,2,0:T(8,128)(2,1)} %bitcast.256, bf16[128,1152,1]{1,0,2:T(8,128)(2,1)} %reshape.136, bf16[4,1,8,128,128]{4,3,2,1,0:T(8,128)(2,1)} %param.7), kind=kOutput, calls=%fused_computation.25 | convolution fusion | flops 302383104 | bytes 3178496 | tf_op jit(solution)/shard_map/dot_general | solution.py:71
  67.0 5.1 %collective-permute-start.6 = (bf16[1,128,128]{2,1,0:T(8,128)(2,1)}, bf16[1,128,128]{2,1,0:T(8,128)(2,1)S(1)}, u32[]{:S(2)}, u32[]{:S(2)}) collective-permute-start(bf16[1,128,128]{2,1,0:T(8,128)(2,1)} %get-tuple-element.23), channel_id=1, source_target_pairs={{0,1},{2,3},{4,5},{6,7},{8,9},{10,11},{12,13},{14,15},{16,17},{18,... | collective-permute-start | bytes 98312 | tf_op jit(solution)/shard_map/ppermute | solution.py:17
  72.2 1.6 fusion.1
  73.7 1.3 copy.27
  78.1 2.7 copy.24
  80.8 3.3 %fusion = f32[128,1152]{0,1:T(8,128)} fusion(bf16[1024,128]{1,0:T(8,128)(2,1)S(1)} %bitcast.258, bf16[144,8,8,128]{3,2,1,0:T(8,128)(2,1)} %bitcast.257), kind=kOutput, calls=%fused_computation.4 | convolution fusion | flops 302137344 | bytes 3211264 | tf_op jit(solution)/shard_map/dot_general | solution.py:66
  84.0 2.1 copy.25
  86.2 1.9 mul.59
  88.1 3.0 %pad_maximum_fusion = f32[1152,512]{1,0:T(8,128)} fusion(f32[1152,128]{1,0:T(8,128)S(1)} %mul.68, f32[1152,128]{1,0:T(8,128)} %mul.65, f32[1152,128]{1,0:T(8,128)} %mul.62, f32[1152,128]{1,0:T(8,128)} %mul.59), kind=kLoop, calls=%fused_computation.16 | loop fusion | flops 1769472 | bytes 4718592 | tf_op jit(solution)/shard_map/concatenate | solution.py:81
  103.5 52.2 %reduce-scatter.2.cloned.1.call-done = f32[72,512]{1,0:T(8,128)} async-done(((f32[1152,512]{1,0:T(8,128)}), f32[72,512]{1,0:T(8,128)}) %reduce-scatter.2.cloned.1.call-update) | async-done | bytes 147472 | tf_op jit(solution)/shard_map/reduce_scatter | solution.py:82
  155.7 1.6 convert_element_type.58
  158.1 34.0 %all-reduce.11.cloned.1.call-done = (bf16[72,512]{1,0:T(8,128)(2,1)}, bf16[1,72,1152]{2,1,0:T(8,128)(2,1)}, bf16[1,72,1152]{2,1,0:T(8,128)(2,1)}, bf16[1,72,1152]{2,1,0:T(8,128)(2,1)}, bf16[1,72,1152]{2,1,0:T(8,128)(2,1)}) async-done(((bf16[72,512]{1,0:T(8,128)(2,1)}, bf16[1,72,1152]{2,1,0:T(8,128)(2,1)}, bf16[1,72,1152]{2,1,0:T(8,128)(2,1)}, bf16[1,72,1152]{2,1,0:T(8,128)(2,1)}, ...) | async-done | bytes 737296 | tf_op jit(solution)/shard_map/psum | solution.py:84
  192.4 2.5 copy.32
  194.9 3.3 %fusion.19 = bf16[1,8,128,128]{3,2,1,0:T(8,128)(2,1)} fusion(bf16[8,128,1152]{1,2,0:T(8,128)(2,1)} %bitcast.250, bf16[128,1152,1]{1,0,2:T(8,128)(2,1)S(1)} %reshape.137), kind=kOutput, calls=%fused_computation.30 | convolution fusion | flops 302120960 | bytes 2916352 | tf_op jit(solution)/shard_map/dot_general | solution.py:71
  198.2 18.3 %all-reduce.9.cloned.1.call-done = (bf16[1,128,128]{2,1,0:T(8,128)(2,1)}, bf16[1,128,128]{2,1,0:T(8,128)(2,1)}, bf16[1,128,128]{2,1,0:T(8,128)(2,1)}, bf16[1,128,128]{2,1,0:T(8,128)(2,1)}) async-done(((bf16[1,128,128]{2,1,0:T(8,128)(2,1)}, bf16[1,128,128]{2,1,0:T(8,128)(2,1)}, bf16[1,128,128]{2,1,0:T(8,128)(2,1)}, bf16[1,128,128]{2,1,0:T(8,128)(2,1)}), (bf16[1,128,128]{2,1,0:T(8,128)(2,1)}, ...) | async-done | bytes 131088 | tf_op jit(solution)/shard_map/psum | solution.py:28
  216.5 40.8 %all-gather.2.cloned.1.call-done = bf16[1152,512]{1,0:T(8,128)(2,1)} async-done(((bf16[72,512]{1,0:T(8,128)(2,1)}), bf16[1152,512]{1,0:T(8,128)(2,1)}) %all-gather.2.cloned.1.call-update) | async-done | bytes 1179664 | tf_op jit(solution)/shard_map/all_gather | solution.py:101
  257.3 2.5 fusion.24
  (106 shorter events, 24.5 us)
Async XLA Ops:
  7.2 9.5 %copy-start.3 = (bf16[4,1,8,128,128]{4,3,2,1,0:T(8,128)(2,1)S(1)}, bf16[4,1,8,128,128]{4,3,2,1,0:T(8,128)(2,1)}, u32[]{:S(2)}) copy-start(bf16[4,1,8,128,128]{4,3,2,1,0:T(8,128)(2,1)} %param.7) | copy-start | bytes 3145732
  7.2 148.5 %reduce-scatter.2.cloned.1.call-start = ((), (), s32[]{:S(2)}) async-start(), calls=%async_computation.1 | async-start | bytes 2506752 | tf_op jit(solution)/shard_map/reduce_scatter | solution.py:82
  9.2 11.0 %collective-permute-start.1 = (bf16[1,128,128]{1,2,0:T(8,128)(2,1)S(1)}, bf16[1,128,128]{1,2,0:T(8,128)(2,1)S(1)}, u32[]{:S(2)}, u32[]{:S(2)}) collective-permute-start(bf16[1,128,128]{1,2,0:T(8,128)(2,1)S(1)} %get-tuple-element.30), channel_id=1, source_target_pairs={{1,0},{3,2},{5,4},{7,6},{9,8},{11,10},{13,12},{15,14},{17,16},{19,... | collective-permute-start | bytes 98312 | tf_op jit(solution)/shard_map/ppermute | solution.py:19
  10.5 9.7 %collective-permute-start = (bf16[1,128,128]{1,2,0:T(8,128)(2,1)S(1)}, bf16[1,128,128]{1,2,0:T(8,128)(2,1)S(1)}, u32[]{:S(2)}, u32[]{:S(2)}) collective-permute-start(bf16[1,128,128]{1,2,0:T(8,128)(2,1)S(1)} %get-tuple-element.29), channel_id=1, source_target_pairs={{0,1},{2,3},{4,5},{6,7},{8,9},{10,11},{12,13},{14,15},{16,17},{18,... | collective-permute-start | bytes 98312 | tf_op jit(solution)/shard_map/ppermute | solution.py:17
  23.1 8.9 %copy-start.8 = (bf16[1,1,8,128,128]{4,3,2,1,0:T(8,128)(2,1)S(1)}, bf16[1,1,8,128,128]{4,3,2,1,0:T(8,128)(2,1)}, u32[]{:S(2)}) copy-start(bf16[1,1,8,128,128]{4,3,2,1,0:T(8,128)(2,1)} %get-tuple-element.18) | copy-start | bytes 786436
  25.6 7.5 %collective-permute-start.3 = (bf16[1,128,128]{2,1,0:T(8,128)(2,1)}, bf16[1,128,128]{2,1,0:T(8,128)(2,1)}, u32[]{:S(2)}, u32[]{:S(2)}) collective-permute-start(bf16[1,128,128]{2,1,0:T(8,128)(2,1)} %get-tuple-element.28), channel_id=1, source_target_pairs={{1,0},{3,2},{5,4},{7,6},{9,8},{11,10},{13,12},{15,14},{17,16},{19,... | collective-permute-start | bytes 98312 | tf_op jit(solution)/shard_map/ppermute | solution.py:19
  26.9 7.0 %collective-permute-start.2 = (bf16[1,128,128]{2,1,0:T(8,128)(2,1)}, bf16[1,128,128]{2,1,0:T(8,128)(2,1)S(1)}, u32[]{:S(2)}, u32[]{:S(2)}) collective-permute-start(bf16[1,128,128]{2,1,0:T(8,128)(2,1)} %get-tuple-element.27), channel_id=1, source_target_pairs={{0,1},{2,3},{4,5},{6,7},{8,9},{10,11},{12,13},{14,15},{16,17},{18,... | collective-permute-start | bytes 98312 | tf_op jit(solution)/shard_map/ppermute | solution.py:17
  41.2 10.0 %copy-start = (bf16[8,128,9,128]{1,0,3,2:T(8,128)(2,1)S(1)}, bf16[8,128,9,128]{1,0,3,2:T(8,128)(2,1)}, u32[]{:S(2)}) copy-start(bf16[8,128,9,128]{1,0,3,2:T(8,128)(2,1)} %copy.28) | copy-start | bytes 7077892
  41.2 10.0 %copy-start.7 = (bf16[1,1,8,128,128]{4,3,2,1,0:T(8,128)(2,1)S(1)}, bf16[1,1,8,128,128]{4,3,2,1,0:T(8,128)(2,1)}, u32[]{:S(2)}) copy-start(bf16[1,1,8,128,128]{4,3,2,1,0:T(8,128)(2,1)} %get-tuple-element.16) | copy-start | bytes 786436
  44.6 10.4 %collective-permute-start.5 = (bf16[1,128,128]{2,1,0:T(8,128)(2,1)}, bf16[1,128,128]{2,1,0:T(8,128)(2,1)}, u32[]{:S(2)}, u32[]{:S(2)}) collective-permute-start(bf16[1,128,128]{2,1,0:T(8,128)(2,1)} %get-tuple-element.26), channel_id=1, source_target_pairs={{1,0},{3,2},{5,4},{7,6},{9,8},{11,10},{13,12},{15,14},{17,16},{19,... | collective-permute-start | bytes 98312 | tf_op jit(solution)/shard_map/ppermute | solution.py:19
  45.9 9.1 %collective-permute-start.4 = (bf16[1,128,128]{2,1,0:T(8,128)(2,1)}, bf16[1,128,128]{2,1,0:T(8,128)(2,1)S(1)}, u32[]{:S(2)}, u32[]{:S(2)}) collective-permute-start(bf16[1,128,128]{2,1,0:T(8,128)(2,1)} %get-tuple-element.25), channel_id=1, source_target_pairs={{0,1},{2,3},{4,5},{6,7},{8,9},{10,11},{12,13},{14,15},{16,17},{18,... | collective-permute-start | bytes 98312 | tf_op jit(solution)/shard_map/ppermute | solution.py:17
  62.3 9.8 %copy-start.1 = (bf16[8,128,9,128]{1,0,3,2:T(8,128)(2,1)S(1)}, bf16[8,128,9,128]{1,0,3,2:T(8,128)(2,1)}, u32[]{:S(2)}) copy-start(bf16[8,128,9,128]{1,0,3,2:T(8,128)(2,1)} %copy.26) | copy-start | bytes 7077892
  62.3 9.8 %copy-start.6 = (bf16[1,1,8,128,128]{4,3,2,1,0:T(8,128)(2,1)S(1)}, bf16[1,1,8,128,128]{4,3,2,1,0:T(8,128)(2,1)}, u32[]{:S(2)}) copy-start(bf16[1,1,8,128,128]{4,3,2,1,0:T(8,128)(2,1)} %get-tuple-element.17) | copy-start | bytes 786436
  65.7 10.2 %collective-permute-start.7 = (bf16[1,128,128]{2,1,0:T(8,128)(2,1)}, bf16[1,128,128]{2,1,0:T(8,128)(2,1)}, u32[]{:S(2)}, u32[]{:S(2)}) collective-permute-start(bf16[1,128,128]{2,1,0:T(8,128)(2,1)} %get-tuple-element.24), channel_id=1, source_target_pairs={{1,0},{3,2},{5,4},{7,6},{9,8},{11,10},{13,12},{15,14},{17,16},{19,... | collective-permute-start | bytes 98312 | tf_op jit(solution)/shard_map/ppermute | solution.py:19
  67.0 8.9 %collective-permute-start.6 = (bf16[1,128,128]{2,1,0:T(8,128)(2,1)}, bf16[1,128,128]{2,1,0:T(8,128)(2,1)S(1)}, u32[]{:S(2)}, u32[]{:S(2)}) collective-permute-start(bf16[1,128,128]{2,1,0:T(8,128)(2,1)} %get-tuple-element.23), channel_id=1, source_target_pairs={{0,1},{2,3},{4,5},{6,7},{8,9},{10,11},{12,13},{14,15},{16,17},{18,... | collective-permute-start | bytes 98312 | tf_op jit(solution)/shard_map/ppermute | solution.py:17
  78.1 2.7 %copy-start.5 = (bf16[1,1,8,128,128]{4,3,2,1,0:T(8,128)(2,1)S(1)}, bf16[1,1,8,128,128]{4,3,2,1,0:T(8,128)(2,1)}, u32[]{:S(2)}) copy-start(bf16[1,1,8,128,128]{4,3,2,1,0:T(8,128)(2,1)} %get-tuple-element.15) | copy-start | bytes 786436
  91.1 0.7 copy-start.9
  91.1 11.6 %copy-start.2 = (bf16[2,72,1152]{2,1,0:T(8,128)(2,1)S(1)}, bf16[2,72,1152]{2,1,0:T(8,128)(2,1)}, u32[]{:S(2)}) copy-start(bf16[2,72,1152]{2,1,0:T(8,128)(2,1)} %param.12) | copy-start | bytes 995332
  91.1 66.2 %copy-start.4 = (bf16[2,128,128]{2,1,0:T(8,128)(2,1)S(1)}, bf16[2,128,128]{2,1,0:T(8,128)(2,1)}, u32[]{:S(2)}) copy-start(bf16[2,128,128]{2,1,0:T(8,128)(2,1)} %param.13) | copy-start | bytes 196612
  91.1 100.9 %all-reduce.11.cloned.1.call-start = ((), (), s32[]{:S(2)}) async-start(), calls=%async_computation.4 | async-start | bytes 1474560 | tf_op jit(solution)/shard_map/psum | solution.py:84
  157.3 59.2 %all-reduce.9.cloned.1.call-start = ((), (), s32[]{:S(2)}) async-start(), calls=%async_computation.3 | async-start | bytes 262144 | tf_op jit(solution)/shard_map/psum | solution.py:28
  158.0 99.3 %all-gather.2.cloned.1.call-start = ((), (), s32[]{:S(2)}) async-start(), calls=%async_computation.2 | async-start | bytes 1253376 | tf_op jit(solution)/shard_map/all_gather | solution.py:101
  194.9 62.4 %copy-start.10 = (bf16[1,72,1152]{2,1,0:T(8,128)(2,1)S(1)}, bf16[1,72,1152]{2,1,0:T(8,128)(2,1)}, u32[]{:S(2)}) copy-start(bf16[1,72,1152]{2,1,0:T(8,128)(2,1)} %get-tuple-element.7) | copy-start | bytes 497668
  194.9 62.4 %copy-start.11 = (bf16[1,72,1152]{2,1,0:T(8,128)(2,1)S(1)}, bf16[1,72,1152]{2,1,0:T(8,128)(2,1)}, u32[]{:S(2)}) copy-start(bf16[1,72,1152]{2,1,0:T(8,128)(2,1)} %get-tuple-element.8) | copy-start | bytes 497668
  194.9 62.4 %copy-start.12 = (bf16[1,72,1152]{2,1,0:T(8,128)(2,1)S(1)}, bf16[1,72,1152]{2,1,0:T(8,128)(2,1)}, u32[]{:S(2)}) copy-start(bf16[1,72,1152]{2,1,0:T(8,128)(2,1)} %get-tuple-element.9) | copy-start | bytes 497668
  194.9 62.4 %copy-start.13 = (bf16[1,72,1152]{2,1,0:T(8,128)(2,1)S(1)}, bf16[1,72,1152]{2,1,0:T(8,128)(2,1)}, u32[]{:S(2)}) copy-start(bf16[1,72,1152]{2,1,0:T(8,128)(2,1)} %get-tuple-element.10) | copy-start | bytes 497668
Sparse Core Ops, SparseCore 0:
  91.2 64.3 reduce-scatter.1
  159.0 32.9 all-reduce.10
  194.6 21.8 all-reduce.8
  218.9 38.3 all-gather.1
where the time goes:
time: 268 us; the launch traced here: 266 us
  waiting for transfers between devices  146 us (54%)
  local copies, waits for them, and re-layouts  37.2 us (14%)
  starting transfers between devices  25.7 us (10%)
  between operations  24.6 us (9%)
  matrix products  20.3 us (8%)
  other arithmetic  12.4 us (5%)
    reduce_scatter x1, waiting for transfers between devices, per_device(): lax.psum_scatter(grad_term, 'dp', scatter_dimension=0, tiled=True)  52.2 us
    all_gather x1, waiting for transfers between devices, per_device(): gathered_piece = lax.all_gather(grad_sum, 'dp', axis=0, tiled=True)  40.8 us
    psum x1, waiting for transfers between devices, per_device(): grad_sum = lax.psum(grad_rows.astype(jnp.bfloat16), 'own')  34 us
    ppermute x4, starting transfers between devices, extended(): lax.ppermute(tail, axis, [(i, (i + 1) % count) for i in range(ends)])  20.4 us
    psum x1, waiting for transfers between devices, from_root(): return lax.psum(block, axis)  18.3 us
    another operation x11, local copies, waits for them, and re-layouts, tap_matrix(): stacked = jnp.stack(pieces, axis=2)  17.2 us
    dot_general x4, matrix products, per_device(): lax.dot_general(tap_rows, kernel, (((1,), (1,)), ((), ())), preferred_ele...  10.5 us
    mul x8, local copies, waits for them, and re-layouts, per_device(): grad_block.reshape(9 * channels, channels) * grad_scale  8.66 us
  transfers between devices with their start and end apart: 12, of which 5 were waited for; matrix products, arithmetic and copies ran while one was open for 8% of the time, Pallas kernels for 0%

commit v1 on v0

--- a/solution.py
+++ b/solution.py
@@ -1,8 +1,11 @@
+import functools
 import math
 
 import jax
 import jax.numpy as jnp
 from jax import lax
+from jax.experimental import pallas as pl
+from jax.experimental.pallas import tpu as pltpu
 from jax.sharding import PartitionSpec as P
 
 
@@ -113,6 +116,347 @@
     return (preconditioned, input_grad)
 
 
+BF = jnp.bfloat16
+F32 = jnp.float32
+MESH = pl.DeviceIdType.MESH
+
+
+def whole_step_kernel(
+    depth_count, reducers, grad_scale,
+    slots_ref, x_ref, w_ref, cot_ref, seg_ref, a_ref, gi_ref,
+    pre_ref, ig_ref,
+    taps, w32, wt, grad32, sent, r1, half, r2, quart, r3, full,
+    edge, halo, a_all, g_all,
+    halo_s, halo_r, ex_s, ex_r, s1, t1, s2, t2, s3, t3, s4, t4, s5, t5, s6, t6,
+):
+    layer_count, num_rows, num_cols, channels = x_ref.shape
+    pixels = num_rows * num_cols
+    dp = lax.axis_index("dp")
+    own = lax.axis_index("own")
+    core = lax.rem(dp, 2)
+    y = lax.rem(dp // 2, 2)
+    z = dp // 4
+    quarter = y * 2 + own
+    slot_count = a_ref.shape[0]
+
+    def core_peer():
+        return (dp + 1 - 2 * core, own)
+
+    def plane_peer(j):
+        other_y = y if j < 2 else 1 - y
+        other_own = own if j % 2 == 0 else 1 - own
+        return ((z * 2 + other_y) * 2 + core, other_own)
+
+    def plane_quarter(j):
+        other_y = y if j < 2 else 1 - y
+        other_own = own if j % 2 == 0 else 1 - own
+        return other_y * 2 + other_own
+
+    def depth_index(j):
+        return lax.rem(z + j, depth_count)
+
+    def depth_peer(j):
+        return ((depth_index(j) * 2 + y) * 2 + core, own)
+
+    def remote(src, dst, send_sem, recv_sem, device):
+        return pltpu.make_async_remote_copy(
+            src_ref=src, dst_ref=dst, send_sem=send_sem, recv_sem=recv_sem,
+            device_id=device, device_id_type=MESH,
+        )
+
+    barrier = pltpu.get_barrier_semaphore()
+    peers = [core_peer()] + [plane_peer(j) for j in range(1, 4)]
+    peers += [depth_peer(j) for j in range(1, depth_count)]
+    for peer in peers:
+        pl.semaphore_signal(barrier, inc=1, device_id=peer, device_id_type=MESH)
+
+    col_index = lax.broadcasted_iota(jnp.int32, (pixels, channels), 0) % num_cols
+
+    def column_shifts(flat):
+        count = flat.shape[0]
+        index = col_index[:count]
+        before = jnp.where(index == num_cols - 1, 0.0, pltpu.roll(flat, count - 1, 0))
+        after = jnp.where(index == 0, 0.0, pltpu.roll(flat, 1, 0))
+        return (before.astype(BF), flat.astype(BF), after.astype(BF))
+
+    def build_taps(buf, grad):
+        flat = grad.astype(F32)
+        for b, piece in enumerate(column_shifts(flat)):
+            taps[buf, 1 : num_rows + 1, :, b * channels : (b + 1) * channels] = piece.reshape(
+                num_rows, num_cols, channels
+            )
+
+    halo_row = (num_rows + 1) * (1 - own)
+    edge_row = (num_rows - 1) * (1 - own)
+
+    def halo_copy(l):
+        return remote(edge.at[l], halo.at[l], halo_s.at[l], halo_r.at[l], (dp, 1 - own))
+
+    def a_copy():
+        place = pl.ds(own * slot_count, slot_count)
+        return remote(a_ref, a_all.at[place], ex_s.at[0], ex_r.at[0], (dp, 1 - own))
+
+    def g_copy():
+        place = pl.ds(own * slot_count, slot_count)
+        return remote(gi_ref, g_all.at[place], ex_s.at[1], ex_r.at[1], (dp, 1 - own))
+
+    def build_weights(l):
+        w32[...] = w_ref[l].astype(F32)
+        for k in range(9):
+            wt[l, :, k * channels : (k + 1) * channels] = w32[
+                pl.ds(k, channels, stride=9), :
+            ].astype(BF)
+
+    last = layer_count - 1
+    labels = seg_ref[...]
+    pixel_weight = jnp.where(labels == 0, 1.0, jnp.where(labels == 1, 0.0, 0.5)).astype(F32)
+    by_column = pixel_weight.T
+    rows = []
+    for r in range(num_rows):
+        rows.append((by_column[:, r : r + 1] * cot_ref[r].astype(F32)).astype(BF))
+    for r in range(num_rows):
+        ig_ref[r] = rows[r]
+    edge[last] = ig_ref[edge_row]
+    pl.semaphore_wait(barrier, len(peers))
+    halo_copy(last).start()
+    a_copy().start()
+    g_copy().start()
+    zero_row = jnp.zeros((num_cols, 3 * channels), BF)
+    for buf in range(2):
+        taps[buf, 0] = zero_row
+        taps[buf, num_rows + 1] = zero_row
+    build_taps(last % 2, ig_ref[...].reshape(pixels, channels))
+    a_all[pl.ds(own * slot_count, slot_count)] = a_ref[...]
+    g_all[pl.ds(own * slot_count, slot_count)] = gi_ref[...]
+
+    def core_copy(l):
+        return remote(sent.at[l, 1 - core], r1.at[l], s1.at[l], t1.at[l], core_peer())
+
+    def plane_copy(l, j):
+        return remote(
+            half.at[l, plane_quarter(j)], r2.at[l, j - 1], s2.at[l, j - 1], t2.at[l, j - 1],
+            plane_peer(j),
+        )
+
+    def depth_copy(l, j):
+        return remote(
+            quart.at[l, lax.min(depth_index(j), reducers - 1)], r3.at[l, j - 1],
+            s3.at[l, j - 1], t3.at[l, j - 1], depth_peer(j),
+        )
+
+    def chunk_at(depth):
+        return (core * 4 + quarter) * reducers + lax.min(depth, reducers - 1)
+
+    def depth_back(l, j, place):
+        return remote(full.at[l, place], full.at[l, place], s4.at[l, j - 1], t4.at[l, j - 1],
+                      depth_peer(j))
+
+    def plane_back(l, j, from_quarter):
+        place = pl.ds((core * 4 + from_quarter) * reducers, reducers)
+        return remote(full.at[l, place], full.at[l, place], s5.at[l, j - 1], t5.at[l, j - 1],
+                      plane_peer(j))
+
+    def core_back(l, from_core):
+        place = pl.ds(from_core * 4 * reducers, 4 * reducers)
+        return remote(full.at[l, place], full.at[l, place], s6.at[l], t6.at[l], core_peer())
+
+    def stage_b(l):
+        core_copy(l).wait()
+        total = sent[l, core].astype(F32) + r1[l].astype(F32)
+        half[l] = total.astype(BF).reshape(half.shape[1:])
+        for j in range(1, 4):
+            plane_copy(l, j).start()
+
+    def stage_c(l):
+        for j in range(1, 4):
+            plane_copy(l, j).wait()
+        total = half[l, quarter].astype(F32)
+        for j in range(3):
+            total = total + r2[l, j].astype(F32)
+        quart[l] = total.astype(BF).reshape(quart.shape[1:])
+        for j in range(1, depth_count):
+            @pl.when(depth_index(j) < reducers)
+            def _():
+                depth_copy(l, j).start()
+
+    def stage_d(l):
+        for j in range(1, depth_count):
+            @pl.when(depth_index(j) < reducers)
+            def _():
+                depth_copy(l, j).wait_send()
+
+        @pl.when(z < reducers)
+        def _():
+            for j in range(1, depth_count):
+                depth_copy(l, j).wait_recv()
+            total = quart[l, lax.min(z, reducers - 1)].astype(F32)
+            for j in range(depth_count - 1):
+                total = total + r3[l, j].astype(F32)
+            full[l, chunk_at(z)] = (total * grad_scale).astype(BF)
+            for j in range(1, depth_count):
+                depth_back(l, j, chunk_at(z)).start()
+
+    def stage_e(l):
+        for j in range(1, depth_count):
+            source = depth_index(depth_count - j)
+
+            @pl.when(source < reducers)
+            def _():
+                depth_back(l, j, chunk_at(source)).wait_recv()
+
+        @pl.when(z < reducers)
+        def _():
+            for j in range(1, depth_count):
+                depth_back(l, j, chunk_at(z)).wait_send()
+        for j in range(1, 4):
+            plane_back(l, j, quarter).start()
+
+    def stage_f(l):
+        for j in range(1, 4):
+            plane_back(l, j, plane_quarter(j)).wait_recv()
+            plane_back(l, j, quarter).wait_send()
+        core_back(l, core).start()
+
+    def stage_h(l):
+        core_back(l, 1 - core).wait_recv()
+        core_back(l, core).wait_send()
+        slot = slots_ref[l]
+        grad_half = full[l].reshape(9 * channels, channels)
+        left = jnp.dot(a_all[slot], grad_half, preferred_element_type=F32)
+        pre_ref[l] = jnp.dot(left.astype(BF), g_all[slot], preferred_element_type=F32)
+
+    stages = [stage_b, stage_c, stage_d, stage_e, stage_f, stage_h]
+    done = {l: 0 for l in range(layer_count)}
+
+    def advance(ready):
+        for l in range(layer_count - 1, ready - 1, -1):
+            if done[l] < len(stages):
+                if stages[done[l]] is stage_h and l == layer_count - 1:
+                    a_copy().wait()
+                    g_copy().wait()
+                stages[done[l]](l)
+                done[l] += 1
+
+    contract_last = (((1,), (1,)), ((), ()))
+    contract_first = (((0,), (0,)), ((), ()))
+    for l in range(layer_count - 1, -1, -1):
+        buf = l % 2
+        build_weights(l)
+        halo_copy(l).wait()
+        for b, piece in enumerate(column_shifts(halo[l].astype(F32))):
+            taps[buf, halo_row, :, b * channels : (b + 1) * channels] = piece
+        if l > 0:
+            side = jnp.zeros((num_cols, channels), F32)
+            for a in range(3):
+                side += lax.dot_general(
+                    taps[buf, edge_row + 2 - a],
+                    wt[l, :, a * 3 * channels : (a + 1) * 3 * channels],
+                    contract_last, preferred_element_type=F32,
+                )
+            edge[l - 1] = jnp.where(x_ref[l, edge_row].astype(F32) > 0, side, 0.0).astype(BF)
+            halo_copy(l - 1).start()
+        side = jnp.zeros((pixels, channels), F32)
+        for a in range(3):
+            side += lax.dot_general(
+                taps[buf, 2 - a : 2 - a + num_rows].reshape(pixels, 3 * channels),
+                wt[l, :, a * 3 * channels : (a + 1) * 3 * channels],
+                contract_last, preferred_element_type=F32,
+            )
+        if l > 0:
+            active = x_ref[l].reshape(pixels, channels).astype(F32) > 0
+            build_taps(1 - buf, jnp.where(active, side, 0.0).astype(BF))
+        else:
+            ig_ref[...] = side.astype(BF).reshape(num_rows, num_cols, channels)
+        if l < last:
+            advance(l + 1)
+        flat_inputs = x_ref[l].reshape(pixels, channels)
+        for a in range(3):
+            block = lax.dot_general(
+                flat_inputs,
+                taps[buf, 2 - a : 2 - a + num_rows].reshape(pixels, 3 * channels),
+                contract_first, preferred_element_type=F32,
+            )
+            for b in range(3):
+                grad32[pl.ds(3 * a + b, channels, stride=9), :] = block[
+                    :, b * channels : (b + 1) * channels
+                ]
+        sent[l] = grad32[...].astype(BF).reshape(sent.shape[1:])
+        core_copy(l).start()
+        if l < last:
+            advance(l + 1)
+    while done[0] < len(stages):
+        advance(0)
+
+
+def reducer_count(quarter_rows, depth_count):
+    for count in range(depth_count, 0, -1):
+        if quarter_rows % (16 * count) == 0:
+            return count
+    return 0
+
+
+def fused_per_device(
+    layer_inputs, weights, top_cotangent, segmentation, layer_slots, a_inverse, g_inverse
+):
+    layer_count = layer_inputs.shape[0]
+    num_rows, num_cols, channels = layer_inputs.shape[2:]
+    taps_rows = 9 * channels
+    data_devices = lax.axis_size("dp")
+    owner_devices = lax.axis_size("own")
+    grad_scale = 1.0 / math.sqrt(data_devices * owner_devices * num_rows * num_cols)
+    depth_count = data_devices // 4
+    quarter_rows = taps_rows // 8
+    reducers = reducer_count(quarter_rows, depth_count)
+    chunk = quarter_rows // reducers
+    slots_total = a_inverse.shape[0] * owner_devices
+    n = layer_count
+    vmem = pl.BlockSpec(memory_space=pltpu.VMEM)
+    dma = pltpu.SemaphoreType.DMA
+    return pl.pallas_call(
+        functools.partial(whole_step_kernel, depth_count, reducers, grad_scale),
+        out_shape=(
+            jax.ShapeDtypeStruct((n, a_inverse.shape[1], channels), F32),
+            jax.ShapeDtypeStruct((num_rows, num_cols, channels), BF),
+        ),
+        in_specs=[pl.BlockSpec(memory_space=pltpu.SMEM)] + [vmem] * 6,
+        out_specs=(vmem, vmem),
+        scratch_shapes=[
+            pltpu.VMEM((2, num_rows + 2, num_cols, 3 * channels), BF),
+            pltpu.VMEM((taps_rows, channels), F32),
+            pltpu.VMEM((n, channels, taps_rows), BF),
+            pltpu.VMEM((taps_rows, channels), F32),
+            pltpu.VMEM((n, 2, taps_rows // 2, channels), BF),
+            pltpu.VMEM((n, taps_rows // 2, channels), BF),
+            pltpu.VMEM((n, 4, quarter_rows, channels), BF),
+            pltpu.VMEM((n, 3, quarter_rows, channels), BF),
+            pltpu.VMEM((n, reducers, chunk, channels), BF),
+            pltpu.VMEM((n, depth_count - 1, chunk, channels), BF),
+            pltpu.VMEM((n, 8 * reducers, chunk, channels), BF),
+            pltpu.VMEM((n, num_cols, channels), BF),
+            pltpu.VMEM((n, num_cols, channels), BF),
+            pltpu.VMEM((slots_total,) + a_inverse.shape[1:], BF),
+            pltpu.VMEM((slots_total,) + g_inverse.shape[1:], BF),
+            dma((n,)), dma((n,)), dma((2,)), dma((2,)),
+            dma((n,)), dma((n,)), dma((n, 3)), dma((n, 3)),
+            dma((n, depth_count - 1)), dma((n, depth_count - 1)),
+            dma((n, depth_count - 1)), dma((n, depth_count - 1)),
+            dma((n, 3)), dma((n, 3)), dma((n,)), dma((n,)),
+        ],
+        compiler_params=pltpu.CompilerParams(
+            collective_id=0, has_side_effects=True, vmem_limit_bytes=48 * 1024 * 1024
+        ),
+        name="whole_step",
+    )(
+        layer_slots, layer_inputs[:, 0], weights, top_cotangent[0], segmentation[0],
+        a_inverse, g_inverse,
+    )
+
+
+def fused_step(*args):
+    preconditioned, input_grad = fused_per_device(*args)
+    return (preconditioned, input_grad[None])
+
+
 def solution(mesh):
     in_specs = (
         P(None, "dp", "own", None, None),
@@ -124,6 +468,8 @@
         P("own", None, None),
     )
     out_specs = (P(None, "dp", None), P("dp", "own", None, None))
+    fits = mesh.shape["own"] == 2 and mesh.shape["dp"] == 16
     return jax.shard_map(
-        per_device, mesh=mesh, in_specs=in_specs, out_specs=out_specs, check_vma=False
+        fused_step if fits else per_device,
+        mesh=mesh, in_specs=in_specs, out_specs=out_specs, check_vma=False,
     )

time: 268 us -> 67.2 us (0.25)
  waiting for transfers between devices: 146 us -> 0 us
  Pallas kernels: 0 us -> 58.2 us
  local copies, waits for them, and re-layouts: 37.2 us -> 7.96 us
  starting transfers between devices: 25.7 us -> 0 us
  between operations: 24.6 us -> 0.66 us
  matrix products: 20.3 us -> 0 us
  other arithmetic: 12.4 us -> 0 us
    pallas_call x0 -> x1, Pallas kernels: none -> 58.2 us  [fused_per_device(): pl.pallas_call(functools.partial(whole_step_kernel, depth_count, reducers...]
    psum x2 -> x0, waiting for transfers between devices: 52.3 us -> none  [the longest x1 34 us: per_device(): grad_sum = lax.psum(grad_rows.astype(jnp.bfloat16), 'own')]
    reduce_scatter x1 -> x0, waiting for transfers between devices: 52.2 us -> none  [per_device(): lax.psum_scatter(grad_term, 'dp', scatter_dimension=0, tiled=True)]
    all_gather x1 -> x0, waiting for transfers between devices: 40.8 us -> none  [per_device(): gathered_piece = lax.all_gather(grad_sum, 'dp', axis=0, tiled=True)]
    ppermute x8 -> x0, starting transfers between devices: 25.6 us -> none  [the longest x4 20.4 us: extended(): lax.ppermute(tail, axis, [(i, (i + 1) % count) for i in range(ends)])]
    dot_general x9 -> x0, matrix products: 20.3 us -> none  [the longest x4 10.5 us: per_device(): lax.dot_general(tap_rows, kernel, (((1,), (1,)), ((), ())), preferred_ele...]
    another operation x15 -> x0, local copies, waits for them, and re-layouts: 20.1 us -> none  [the longest x11 17.2 us: tap_matrix(): stacked = jnp.stack(pieces, axis=2)]
    mul x8 -> x0, local copies, waits for them, and re-layouts: 8.66 us -> none  [per_device(): grad_block.reshape(9 * channels, channels) * grad_scale]
  transfers between devices with their start and end apart: 12 -> 0, of which waited for: 5 -> 0; matrix products, arithmetic and copies ran while one was open for 8% -> 0% of each run, Pallas kernels for 0% -> 0%
where the time goes in v1:
time: 67.2 us; the launch traced here: 66.8 us
  Pallas kernels  58.2 us (87%)
  local copies, waits for them, and re-layouts  7.96 us (12%)
    pallas_call x1, Pallas kernels, fused_per_device(): pl.pallas_call(functools.partial(whole_step_kernel, depth_count, reducers...  58.2 us
    unnamed x16, local copies, waits for them, and re-layouts  7.96 us

profile of v1, /device:TPU:0, one launch (start us, length us, event | category | flops | bytes accessed | tf_op | source)
XLA Modules:
  0.0 66.8 jit_solution(1986310444420380226)
XLA Ops:
  0.6 0.0 copy-start
  0.6 1.3 %copy-done = bf16[4,1152,128]{2,1,0:T(8,128)(2,1)S(1)} copy-done((bf16[4,1152,128]{2,1,0:T(8,128)(2,1)S(1)}, bf16[4,1152,128]{2,1,0:T(8,128)(2,1)}, u32[]{:S(2)}) %copy-start) | copy-done | bytes 1179672
  1.9 0.0 copy-start.1
  1.9 1.2 %copy-done.1 = bf16[4,1,8,128,128]{4,3,2,1,0:T(8,128)(2,1)S(1)} copy-done((bf16[4,1,8,128,128]{4,3,2,1,0:T(8,128)(2,1)S(1)}, bf16[4,1,8,128,128]{4,3,2,1,0:T(8,128)(2,1)}, u32[]{:S(2)}) %copy-start.1) | copy-done | bytes 1048600
  3.1 0.0 copy-start.2
  3.1 1.0 %copy-done.2 = bf16[2,72,1152]{2,1,0:T(8,128)(2,1)S(1)} copy-done((bf16[2,72,1152]{2,1,0:T(8,128)(2,1)S(1)}, bf16[2,72,1152]{2,1,0:T(8,128)(2,1)}, u32[]{:S(2)}) %copy-start.2) | copy-done | bytes 331800
  4.1 0.0 copy-start.3
  4.1 0.9 %copy-done.3 = bf16[1,8,128,128]{3,2,1,0:T(8,128)(2,1)S(1)} copy-done((bf16[1,8,128,128]{3,2,1,0:T(8,128)(2,1)S(1)}, bf16[1,8,128,128]{3,2,1,0:T(8,128)(2,1)}, u32[]{:S(2)}) %copy-start.3) | copy-done | bytes 262168
  5.1 0.0 copy-start.4
  5.1 0.8 %copy-done.4 = bf16[2,128,128]{2,1,0:T(8,128)(2,1)S(1)} copy-done((bf16[2,128,128]{2,1,0:T(8,128)(2,1)S(1)}, bf16[2,128,128]{2,1,0:T(8,128)(2,1)}, u32[]{:S(2)}) %copy-start.4) | copy-done | bytes 65560
  5.9 0.0 copy-start.5
  5.9 0.7 %copy-done.5 = s32[1,8,128]{2,1,0:T(8,128)S(1)} copy-done((s32[1,8,128]{2,1,0:T(8,128)S(1)}, s32[1,8,128]{2,1,0:T(8,128)}, u32[]{:S(2)}) %copy-start.5) | copy-done | bytes 4120
  6.6 0.0 copy-start.6
  6.6 0.7 copy-done.6
  7.2 58.2 %whole_step.1 = (f32[4,72,128]{2,1,0:T(8,128)S(1)}, bf16[8,128,128]{2,1,0:T(8,128)(2,1)S(1)}) custom-call(s32[4]{0:T(128)S(1)} %copy-done.6, bf16[4,8,128,128]{3,2,1,0:T(8,128)(2,1)S(1)} %bitcast.4, bf16[4,1152,128]{2,1,0:T(8,128)(2,1)S(1)} %copy-done, bf16[8,128,128]{2,1,0:T(8,128)(2,1)S(1)} %bitcast.5, s32[8,128]{1,0:T(8,128)S(1)} %bitcast.7, ...), custom_call_target="tpu_custom_call" | custom-call | tf_op jit(solution)/shard_map/whole_step/pallas_call | solution.py:415
  65.5 0.7 copy.11
  66.1 0.7 %copy.12 = bf16[1,8,128,128]{3,2,1,0:T(8,128)(2,1)} copy(bf16[1,8,128,128]{3,2,1,0:T(8,128)(2,1)S(1)} %bitcast.6) | data formatting | bytes 524288
Async XLA Ops:
  0.6 1.3 %copy-start = (bf16[4,1152,128]{2,1,0:T(8,128)(2,1)S(1)}, bf16[4,1152,128]{2,1,0:T(8,128)(2,1)}, u32[]{:S(2)}) copy-start(bf16[4,1152,128]{2,1,0:T(8,128)(2,1)} %w_ref.1) | copy-start | bytes 3538948
  1.9 1.2 %copy-start.1 = (bf16[4,1,8,128,128]{4,3,2,1,0:T(8,128)(2,1)S(1)}, bf16[4,1,8,128,128]{4,3,2,1,0:T(8,128)(2,1)}, u32[]{:S(2)}) copy-start(bf16[4,1,8,128,128]{4,3,2,1,0:T(8,128)(2,1)} %param.7) | copy-start | bytes 3145732
  3.1 1.0 %copy-start.2 = (bf16[2,72,1152]{2,1,0:T(8,128)(2,1)S(1)}, bf16[2,72,1152]{2,1,0:T(8,128)(2,1)}, u32[]{:S(2)}) copy-start(bf16[2,72,1152]{2,1,0:T(8,128)(2,1)} %a_ref.1) | copy-start | bytes 995332
  4.1 0.9 %copy-start.3 = (bf16[1,8,128,128]{3,2,1,0:T(8,128)(2,1)S(1)}, bf16[1,8,128,128]{3,2,1,0:T(8,128)(2,1)}, u32[]{:S(2)}) copy-start(bf16[1,8,128,128]{3,2,1,0:T(8,128)(2,1)} %param.9) | copy-start | bytes 786436
  5.1 0.8 %copy-start.4 = (bf16[2,128,128]{2,1,0:T(8,128)(2,1)S(1)}, bf16[2,128,128]{2,1,0:T(8,128)(2,1)}, u32[]{:S(2)}) copy-start(bf16[2,128,128]{2,1,0:T(8,128)(2,1)} %gi_ref.1) | copy-start | bytes 196612
  5.9 0.7 %copy-start.5 = (s32[1,8,128]{2,1,0:T(8,128)S(1)}, s32[1,8,128]{2,1,0:T(8,128)}, u32[]{:S(2)}) copy-start(s32[1,8,128]{2,1,0:T(8,128)} %param.10) | copy-start | bytes 12292
  6.6 0.7 copy-start.6

commit v2 on v1

--- a/solution.py
+++ b/solution.py
@@ -123,10 +123,10 @@
 
 def whole_step_kernel(
     depth_count, reducers, grad_scale,
-    slots_ref, x_ref, w_ref, cot_ref, seg_ref, a_ref, gi_ref,
+    slots_ref, x_hbm, w_hbm, cot_hbm, seg_hbm, a_hbm, gi_hbm,
     pre_ref, ig_ref,
     taps, w32, wt, grad32, sent, r1, half, r2, quart, r3, full,
-    edge, halo, a_all, g_all,
+    edge, halo, a_all, g_all, x_ref, w_ref, cot_ref, seg_ref, load,
     halo_s, halo_r, ex_s, ex_r, s1, t1, s2, t2, s3, t3, s4, t4, s5, t5, s6, t6,
 ):
     layer_count, num_rows, num_cols, channels = x_ref.shape
@@ -137,7 +137,8 @@
     y = lax.rem(dp // 2, 2)
     z = dp // 4
     quarter = y * 2 + own
-    slot_count = a_ref.shape[0]
+    slot_count = a_hbm.shape[0]
+    held = pl.ds(own * slot_count, slot_count)
 
     def core_peer():
         return (dp + 1 - 2 * core, own)
@@ -163,6 +164,28 @@
             src_ref=src, dst_ref=dst, send_sem=send_sem, recv_sem=recv_sem,
             device_id=device, device_id_type=MESH,
         )
+
+    last = layer_count - 1
+    cot_load = pltpu.make_async_copy(cot_hbm, cot_ref, load.at[0])
+    seg_load = pltpu.make_async_copy(seg_hbm, seg_ref, load.at[1])
+    a_load = pltpu.make_async_copy(a_hbm, a_all.at[held], load.at[2])
+    g_load = pltpu.make_async_copy(gi_hbm, g_all.at[held], load.at[3])
+
+    def x_load(l):
+        return pltpu.make_async_copy(x_hbm.at[l], x_ref.at[l], load.at[4 + l])
+
+    def w_load(l):
+        return pltpu.make_async_copy(w_hbm.at[l], w_ref.at[l], load.at[4 + layer_count + l])
+
+    seg_load.start()
+    cot_load.start()
+    w_load(last).start()
+    x_load(last).start()
+    a_load.start()
+    g_load.start()
+    for l in range(last - 1, -1, -1):
+        w_load(l).start()
+        x_load(l).start()
 
     barrier = pltpu.get_barrier_semaphore()
     peers = [core_peer()] + [plane_peer(j) for j in range(1, 4)]
@@ -192,13 +215,16 @@
     def halo_copy(l):
         return remote(edge.at[l], halo.at[l], halo_s.at[l], halo_r.at[l], (dp, 1 - own))
 
-    def a_copy():
-        place = pl.ds(own * slot_count, slot_count)
-        return remote(a_ref, a_all.at[place], ex_s.at[0], ex_r.at[0], (dp, 1 - own))
+    def a_copy(k):
+        place = a_all.at[own * slot_count + k]
+        return remote(place, place, ex_s.at[k], ex_r.at[k], (dp, 1 - own))
 
     def g_copy():
-        place = pl.ds(own * slot_count, slot_count)
-        return remote(gi_ref, g_all.at[place], ex_s.at[1], ex_r.at[1], (dp, 1 - own))
+        return remote(g_all.at[held], g_all.at[held], ex_s.at[slot_count], ex_r.at[slot_count],
+                      (dp, 1 - own))
+
+    def factor_copies():
+        return [a_copy(k) for k in range(slot_count)] + [g_copy()]
 
     def build_weights(l):
         w32[...] = w_ref[l].astype(F32)
@@ -207,7 +233,8 @@
                 pl.ds(k, channels, stride=9), :
             ].astype(BF)
 
-    last = layer_count - 1
+    seg_load.wait()
+    cot_load.wait()
     labels = seg_ref[...]
     pixel_weight = jnp.where(labels == 0, 1.0, jnp.where(labels == 1, 0.0, 0.5)).astype(F32)
     by_column = pixel_weight.T
@@ -219,15 +246,11 @@
     edge[last] = ig_ref[edge_row]
     pl.semaphore_wait(barrier, len(peers))
     halo_copy(last).start()
-    a_copy().start()
-    g_copy().start()
     zero_row = jnp.zeros((num_cols, 3 * channels), BF)
     for buf in range(2):
         taps[buf, 0] = zero_row
         taps[buf, num_rows + 1] = zero_row
     build_taps(last % 2, ig_ref[...].reshape(pixels, channels))
-    a_all[pl.ds(own * slot_count, slot_count)] = a_ref[...]
-    g_all[pl.ds(own * slot_count, slot_count)] = gi_ref[...]
 
     def core_copy(l):
         return remote(sent.at[l, 1 - core], r1.at[l], s1.at[l], t1.at[l], core_peer())
@@ -325,23 +348,64 @@
         left = jnp.dot(a_all[slot], grad_half, preferred_element_type=F32)
         pre_ref[l] = jnp.dot(left.astype(BF), g_all[slot], preferred_element_type=F32)
 
-    stages = [stage_b, stage_c, stage_d, stage_e, stage_f, stage_h]
-    done = {l: 0 for l in range(layer_count)}
-
-    def advance(ready):
-        for l in range(layer_count - 1, ready - 1, -1):
-            if done[l] < len(stages):
-                if stages[done[l]] is stage_h and l == layer_count - 1:
-                    a_copy().wait()
-                    g_copy().wait()
-                stages[done[l]](l)
-                done[l] += 1
+    def factors_here(l):
+        if l == last:
+            for copy in factor_copies():
+                copy.wait()
+
+    stages = [
+        (1.3, stage_b), (5.5, stage_c), (8.8, stage_d), (12.0, stage_e), (16.0, stage_f),
+        (17.2, factors_here), (17.2, stage_h),
+    ]
+    pending = []
+
+    def launch(l, now):
+        core_copy(l).start()
+        pending.extend((now + delay, -l, place) for place, (delay, _) in enumerate(stages))
+        pending.sort(key=lambda event: (event[0], event[1], event[2]))
+
+    def run_until(now):
+        while pending and pending[0][0] <= now:
+            _, minus_l, place = pending.pop(0)
+            stages[place][1](-minus_l)
 
     contract_last = (((1,), (1,)), ((), ()))
     contract_first = (((0,), (0,)), ((), ()))
-    for l in range(layer_count - 1, -1, -1):
+
+    def tap_rows(buf, a):
+        return taps[buf, 2 - a : 2 - a + num_rows].reshape(pixels, 3 * channels)
+
+    def bulk_side(l):
+        side = jnp.zeros((pixels, channels), F32)
+        for a in range(3):
+            side += lax.dot_general(
+                tap_rows(l % 2, a), wt[l, :, a * 3 * channels : (a + 1) * 3 * channels],
+                contract_last, preferred_element_type=F32,
+            )
+        return side
+
+    def weight_grad(l):
+        flat_inputs = x_ref[l].reshape(pixels, channels)
+        for a in range(3):
+            block = lax.dot_general(
+                flat_inputs, tap_rows(l % 2, a), contract_first, preferred_element_type=F32
+            )
+            for b in range(3):
+                grad32[pl.ds(3 * a + b, channels, stride=9), :] = block[
+                    :, b * channels : (b + 1) * channels
+                ]
+        sent[l] = grad32[...].astype(BF).reshape(sent.shape[1:])
+
+    late_copies = factor_copies()
+    for l in range(last, -1, -1):
         buf = l % 2
+        now = 4.0 * (last - l)
+        w_load(l).wait()
         build_weights(l)
+        if l == last:
+            a_load.wait()
+            g_load.wait()
+        x_load(l).wait()
         halo_copy(l).wait()
         for b, piece in enumerate(column_shifts(halo[l].astype(F32))):
             taps[buf, halo_row, :, b * channels : (b + 1) * channels] = piece
@@ -355,37 +419,24 @@
                 )
             edge[l - 1] = jnp.where(x_ref[l, edge_row].astype(F32) > 0, side, 0.0).astype(BF)
             halo_copy(l - 1).start()
-        side = jnp.zeros((pixels, channels), F32)
-        for a in range(3):
-            side += lax.dot_general(
-                taps[buf, 2 - a : 2 - a + num_rows].reshape(pixels, 3 * channels),
-                wt[l, :, a * 3 * channels : (a + 1) * 3 * channels],
-                contract_last, preferred_element_type=F32,
-            )
-        if l > 0:
+            if late_copies:
+                late_copies.pop(0).start()
+            run_until(now + 0.8)
             active = x_ref[l].reshape(pixels, channels).astype(F32) > 0
-            build_taps(1 - buf, jnp.where(active, side, 0.0).astype(BF))
+            build_taps(1 - buf, jnp.where(active, bulk_side(l), 0.0).astype(BF))
+            run_until(now + 2.2)
+            weight_grad(l)
+            launch(l, now + 4.0)
+            run_until(now + 4.0)
         else:
-            ig_ref[...] = side.astype(BF).reshape(num_rows, num_cols, channels)
-        if l < last:
-            advance(l + 1)
-        flat_inputs = x_ref[l].reshape(pixels, channels)
-        for a in range(3):
-            block = lax.dot_general(
-                flat_inputs,
-                taps[buf, 2 - a : 2 - a + num_rows].reshape(pixels, 3 * channels),
-                contract_first, preferred_element_type=F32,
-            )
-            for b in range(3):
-                grad32[pl.ds(3 * a + b, channels, stride=9), :] = block[
-                    :, b * channels : (b + 1) * channels
-                ]
-        sent[l] = grad32[...].astype(BF).reshape(sent.shape[1:])
-        core_copy(l).start()
-        if l < last:
-            advance(l + 1)
-    while done[0] < len(stages):
-        advance(0)
+            for copy in late_copies:
+                copy.start()
+            run_until(now + 0.8)
+            weight_grad(l)
+            launch(l, now + 2.6)
+            run_until(now + 2.6)
+            ig_ref[...] = bulk_side(l).astype(BF).reshape(num_rows, num_cols, channels)
+    run_until(float("inf"))
 
 
 def reducer_count(quarter_rows, depth_count):
@@ -418,7 +469,7 @@
             jax.ShapeDtypeStruct((n, a_inverse.shape[1], channels), F32),
             jax.ShapeDtypeStruct((num_rows, num_cols, channels), BF),
         ),
-        in_specs=[pl.BlockSpec(memory_space=pltpu.SMEM)] + [vmem] * 6,
+        in_specs=[pl.BlockSpec(memory_space=pltpu.SMEM)] + [pl.BlockSpec(memory_space=pltpu.HBM)] * 6,
         out_specs=(vmem, vmem),
         scratch_shapes=[
             pltpu.VMEM((2, num_rows + 2, num_cols, 3 * channels), BF),
@@ -436,7 +487,12 @@
             pltpu.VMEM((n, num_cols, channels), BF),
             pltpu.VMEM((slots_total,) + a_inverse.shape[1:], BF),
             pltpu.VMEM((slots_total,) + g_inverse.shape[1:], BF),
-            dma((n,)), dma((n,)), dma((2,)), dma((2,)),
+            pltpu.VMEM((n, num_rows, num_cols, channels), BF),
+            pltpu.VMEM((n, taps_rows, channels), BF),
+            pltpu.VMEM((num_rows, num_cols, channels), BF),
+            pltpu.VMEM((num_rows, num_cols), jnp.int32),
+            dma((4 + 2 * n,)),
+            dma((n,)), dma((n,)), dma((a_inverse.shape[0] + 1,)), dma((a_inverse.shape[0] + 1,)),
             dma((n,)), dma((n,)), dma((n, 3)), dma((n, 3)),
             dma((n, depth_count - 1)), dma((n, depth_count - 1)),
             dma((n, depth_count - 1)), dma((n, depth_count - 1)),

time: 67.2 us -> 55.4 us (0.82)
  Pallas kernels: 58.2 us -> 46.4 us
    pallas_call x1, Pallas kernels: 58.2 us -> 46.4 us  [fused_per_device(): pl.pallas_call(functools.partial(whole_step_kernel, depth_count, reducers...]
where the time goes in v2:
time: 55.4 us; the launch traced here: 55.1 us
  Pallas kernels  46.4 us (84%)
  local copies, waits for them, and re-layouts  7.96 us (14%)
  between operations  0.66 us (1%)
    pallas_call x1, Pallas kernels, fused_per_device(): pl.pallas_call(functools.partial(whole_step_kernel, depth_count, reducers...  46.4 us
    unnamed x16, local copies, waits for them, and re-layouts  7.96 us

profile of v2, /device:TPU:0, one launch (start us, length us, event | category | flops | bytes accessed | tf_op | source)
XLA Modules:
  0.0 55.1 jit_solution(8285765670140739267)
XLA Ops:
  0.6 0.0 copy-start
  0.6 1.3 %copy-done = bf16[4,1152,128]{2,1,0:T(8,128)(2,1)S(1)} copy-done((bf16[4,1152,128]{2,1,0:T(8,128)(2,1)S(1)}, bf16[4,1152,128]{2,1,0:T(8,128)(2,1)}, u32[]{:S(2)}) %copy-start) | copy-done | bytes 1179672
  1.9 0.0 copy-start.1
  1.9 1.2 %copy-done.1 = bf16[4,1,8,128,128]{4,3,2,1,0:T(8,128)(2,1)S(1)} copy-done((bf16[4,1,8,128,128]{4,3,2,1,0:T(8,128)(2,1)S(1)}, bf16[4,1,8,128,128]{4,3,2,1,0:T(8,128)(2,1)}, u32[]{:S(2)}) %copy-start.1) | copy-done | bytes 1048600
  3.1 0.0 copy-start.2
  3.1 1.0 %copy-done.2 = bf16[2,72,1152]{2,1,0:T(8,128)(2,1)S(1)} copy-done((bf16[2,72,1152]{2,1,0:T(8,128)(2,1)S(1)}, bf16[2,72,1152]{2,1,0:T(8,128)(2,1)}, u32[]{:S(2)}) %copy-start.2) | copy-done | bytes 331800
  4.1 0.0 copy-start.3
  4.1 0.9 %copy-done.3 = bf16[1,8,128,128]{3,2,1,0:T(8,128)(2,1)S(1)} copy-done((bf16[1,8,128,128]{3,2,1,0:T(8,128)(2,1)S(1)}, bf16[1,8,128,128]{3,2,1,0:T(8,128)(2,1)}, u32[]{:S(2)}) %copy-start.3) | copy-done | bytes 262168
  5.1 0.0 copy-start.4
  5.1 0.8 %copy-done.4 = bf16[2,128,128]{2,1,0:T(8,128)(2,1)S(1)} copy-done((bf16[2,128,128]{2,1,0:T(8,128)(2,1)S(1)}, bf16[2,128,128]{2,1,0:T(8,128)(2,1)}, u32[]{:S(2)}) %copy-start.4) | copy-done | bytes 65560
  5.9 0.0 copy-start.5
  5.9 0.7 %copy-done.5 = s32[1,8,128]{2,1,0:T(8,128)S(1)} copy-done((s32[1,8,128]{2,1,0:T(8,128)S(1)}, s32[1,8,128]{2,1,0:T(8,128)}, u32[]{:S(2)}) %copy-start.5) | copy-done | bytes 4120
  6.6 0.0 copy-start.6
  6.6 0.7 %copy-done.6 = s32[4]{0:T(128)S(1)} copy-done((s32[4]{0:T(128)S(1)}, s32[4]{0:T(128)}, u32[]{:S(2)}) %copy-start.6) | copy-done | bytes 40
  7.2 46.4 %whole_step.1 = (f32[4,72,128]{2,1,0:T(8,128)S(1)}, bf16[8,128,128]{2,1,0:T(8,128)(2,1)S(1)}) custom-call(s32[4]{0:T(128)S(1)} %copy-done.6, bf16[4,8,128,128]{3,2,1,0:T(8,128)(2,1)S(1)} %bitcast.4, bf16[4,1152,128]{2,1,0:T(8,128)(2,1)S(1)} %copy-done, bf16[8,128,128]{2,1,0:T(8,128)(2,1)S(1)} %bitcast.5, s32[8,128]{1,0:T(8,128)S(1)} %bitcast.7, ...), custom_call_target="tpu_custom_call" | custom-call | tf_op jit(solution)/shard_map/whole_step/pallas_call | solution.py:466
  53.7 0.7 %copy.11 = f32[4,72,128]{2,1,0:T(8,128)} copy(f32[4,72,128]{2,1,0:T(8,128)S(1)} %get-tuple-element.8) | data formatting | bytes 294912
  54.4 0.7 %copy.12 = bf16[1,8,128,128]{3,2,1,0:T(8,128)(2,1)} copy(bf16[1,8,128,128]{3,2,1,0:T(8,128)(2,1)S(1)} %bitcast.6) | data formatting | bytes 524288
Async XLA Ops:
  0.6 1.3 %copy-start = (bf16[4,1152,128]{2,1,0:T(8,128)(2,1)S(1)}, bf16[4,1152,128]{2,1,0:T(8,128)(2,1)}, u32[]{:S(2)}) copy-start(bf16[4,1152,128]{2,1,0:T(8,128)(2,1)} %w_hbm.1) | copy-start | bytes 3538948
  1.9 1.2 %copy-start.1 = (bf16[4,1,8,128,128]{4,3,2,1,0:T(8,128)(2,1)S(1)}, bf16[4,1,8,128,128]{4,3,2,1,0:T(8,128)(2,1)}, u32[]{:S(2)}) copy-start(bf16[4,1,8,128,128]{4,3,2,1,0:T(8,128)(2,1)} %param.7) | copy-start | bytes 3145732
  3.1 1.0 %copy-start.2 = (bf16[2,72,1152]{2,1,0:T(8,128)(2,1)S(1)}, bf16[2,72,1152]{2,1,0:T(8,128)(2,1)}, u32[]{:S(2)}) copy-start(bf16[2,72,1152]{2,1,0:T(8,128)(2,1)} %a_hbm.1) | copy-start | bytes 995332
  4.1 0.9 %copy-start.3 = (bf16[1,8,128,128]{3,2,1,0:T(8,128)(2,1)S(1)}, bf16[1,8,128,128]{3,2,1,0:T(8,128)(2,1)}, u32[]{:S(2)}) copy-start(bf16[1,8,128,128]{3,2,1,0:T(8,128)(2,1)} %param.9) | copy-start | bytes 786436
  5.1 0.8 %copy-start.4 = (bf16[2,128,128]{2,1,0:T(8,128)(2,1)S(1)}, bf16[2,128,128]{2,1,0:T(8,128)(2,1)}, u32[]{:S(2)}) copy-start(bf16[2,128,128]{2,1,0:T(8,128)(2,1)} %gi_hbm.1) | copy-start | bytes 196612
  5.9 0.7 %copy-start.5 = (s32[1,8,128]{2,1,0:T(8,128)S(1)}, s32[1,8,128]{2,1,0:T(8,128)}, u32[]{:S(2)}) copy-start(s32[1,8,128]{2,1,0:T(8,128)} %param.10) | copy-start | bytes 12292
  6.6 0.7 %copy-start.6 = (s32[4]{0:T(128)S(1)}, s32[4]{0:T(128)}, u32[]{:S(2)}) copy-start(s32[4]{0:T(128)} %slots_ref.1) | copy-start | bytes 52

commit v3 on v2

--- a/solution.py
+++ b/solution.py
@@ -499,7 +499,7 @@
             dma((n, 3)), dma((n, 3)), dma((n,)), dma((n,)),
         ],
         compiler_params=pltpu.CompilerParams(
-            collective_id=0, has_side_effects=True, vmem_limit_bytes=48 * 1024 * 1024
+            collective_id=0, has_side_effects=True, vmem_limit_bytes=60 * 1024 * 1024
         ),
         name="whole_step",
     )(

time: 55.4 us -> 50.8 us (0.917)
  local copies, waits for them, and re-layouts: 7.96 us -> 3.25 us
    unnamed x16 -> x2, local copies, waits for them, and re-layouts: 7.96 us -> 3.25 us
where the time goes in v3:
time: 50.8 us; the launch traced here: 50.6 us
  Pallas kernels  46.7 us (92%)
  local copies, waits for them, and re-layouts  3.25 us (6%)
  between operations  0.64 us (1%)
    pallas_call x1, Pallas kernels, fused_per_device(): pl.pallas_call(functools.partial(whole_step_kernel, depth_count, reducers...  46.7 us
    unnamed x2, local copies, waits for them, and re-layouts  3.25 us

profile of v3, /device:TPU:0, one launch (start us, length us, event | category | flops | bytes accessed | tf_op | source)
XLA Modules:
  0.0 50.6 jit_solution(2152516085911626168)
XLA Ops:
  0.6 46.7 %whole_step.1 = (f32[4,72,128]{2,1,0:T(8,128)}, bf16[8,128,128]{2,1,0:T(8,128)(2,1)}) custom-call(s32[4]{0:T(128)} %slots_ref.1, bf16[4,8,128,128]{3,2,1,0:T(8,128)(2,1)} %bitcast.4, bf16[4,1152,128]{2,1,0:T(8,128)(2,1)} %w_hbm.1, bf16[8,128,128]{2,1,0:T(8,128)(2,1)} %bitcast.5, s32[8,128]{1,0:T(8,128)} %bitcast.7, bf16[2,72,1152]{2,1,0:T(8,128)(2,1)} %a_hbm.1, ...), custom_call_target="tpu_custom_call" | custom-call | tf_op jit(solution)/shard_map/whole_step/pallas_call | solution.py:466
  47.3 1.6 %copy.11 = f32[4,72,128]{2,1,0:T(8,128)} copy(f32[4,72,128]{2,1,0:T(8,128)} %get-tuple-element.8) | data formatting | bytes 294912
  48.9 1.7 %copy.12 = bf16[1,8,128,128]{3,2,1,0:T(8,128)(2,1)} copy(bf16[1,8,128,128]{3,2,1,0:T(8,128)(2,1)} %bitcast.6) | data formatting | bytes 524288
